TPU v7x, 512 devices: a whole 4x4x16 slice. The times are simulated.
512 devices in a mesh: dp: 32 (over x, y, core), expert: 16 (over z).
Axes of the slice: x: 4, y: 4, z: 16, core: 2. Of those that a mesh axis runs over, the one named last changes fastest.
Arguments:
- tokens: bfloat16 [65536, 7168], P(('dp', 'expert')), may hold values from -6 to 6
- route_ids: int32 [65536, 8], P(('dp', 'expert')), may hold values from 0 to 255, as said below
- route_gates: float32 [65536, 8], P(('dp', 'expert')), may hold values from 0.1 to 1
- gate_up: bfloat16 [2, 7168, 2048], P(None, 'dp', 'expert'), may hold values from -0.0625 to 0.0625
- down_weight: bfloat16 [2048, 7168], P('expert', 'dp'), may hold values from -0.125 to 0.125
Outputs:
- mixed: bfloat16 [65536, 7168], P(('dp', 'expert'))
Inputs may be any that keep to these rules, and one draw needn't show every extreme that they name: `route_ids`: each token names 8 different experts. Among the 128 rows of one device, each expert below 1 is named by 1 to 12 rows; for each such expert, in every draw some run of 16 consecutive devices' blocks (aligned at multiples of 16) has exactly 12 rows naming it in every block.
All inputs are finite; a program needn't handle non-finite values.
Results may differ from a plain program's by a relative error of at most 0.0057.
Values may be sent and summed in bfloat16 or wider, within the bound.
No kernel may reach another device: no remote copies, remote signals or barrier semaphores. Data moves between devices by JAX's collectives and lax.ppermute only.
A program may use at most 64 MiB of HBM per device.

v0:
```python
import jax
import jax.numpy as jnp
from jax import lax
from jax.sharding import PartitionSpec as P

EXPERTS = 1
CAP = 12


def body(tokens, route_ids, route_gates, gate_up, down_weight):
    model_width = tokens.shape[1]
    matches = route_ids == 0
    routed = jnp.any(matches, axis=1)
    weight = jnp.sum(jnp.where(matches, route_gates, 0.0), axis=1)
    places = jnp.cumsum(routed.astype(jnp.int32)) - 1
    capacity_ids = jnp.arange(CAP, dtype=jnp.int32)
    packing = (routed[None, :] & (places[None, :] == capacity_ids[:, None])).astype(jnp.bfloat16)
    packed = jnp.dot(packing, tokens, preferred_element_type=jnp.float32).astype(jnp.bfloat16)
    dispatched = lax.all_gather(packed, "expert", axis=0, tiled=True)
    gu = lax.all_gather(gate_up, "dp", axis=1, tiled=True)
    dn = lax.all_gather(down_weight, "dp", axis=1, tiled=True)
    projected = jnp.einsum("rd,gdf->grf", dispatched, gu, preferred_element_type=jnp.float32)
    hidden = (jax.nn.silu(projected[0]) * projected[1]).astype(jnp.bfloat16)
    partial_value = jnp.dot(hidden, dn, preferred_element_type=jnp.float32).astype(jnp.bfloat16)
    summed = lax.psum_scatter(partial_value, "expert", scatter_dimension=0, tiled=True)
    selector = routed[:, None] & (places[:, None] == capacity_ids[None, :])
    scaled = jnp.where(selector, weight[:, None], 0.0)
    mixed = jnp.dot(
        scaled,
        summed.astype(jnp.float32),
        precision=lax.Precision.HIGHEST,
        preferred_element_type=jnp.float32,
    )
    return mixed.astype(jnp.bfloat16)


def solution(mesh):
    return jax.shard_map(
        body,
        mesh=mesh,
        in_specs=(
            P(("dp", "expert"), None),
            P(("dp", "expert"), None),
            P(("dp", "expert"), None),
            P(None, "dp", "expert"),
            P("expert", "dp"),
        ),
        out_specs=P(("dp", "expert"), None),
        check_vma=False,
    )
```

profile of v0, /device:TPU:96, one launch (start us, length us, event | category | flops | bytes accessed | tf_op | source)
XLA Modules:
  0.0 334.5 jit_solution(3972932187216507593)
XLA Ops:
  6.5 0.0 copy-start
  6.5 0.0 all-gather.9.cloned.1.call-start
  6.5 0.9 select_reduce_fusion
  7.4 0.1 copy.8
  7.5 0.2 reduce-window.7
  7.7 0.1 add_reduce_fusion
  7.8 0.3 copy-done
  8.1 1.0 fusion.1
  9.1 0.0 all-gather.9.cloned.1.call-update
  9.1 0.0 all-gather.5.cloned.1.call-start
  9.2 0.7 all-gather.5.cloned.1.call-update
  9.9 0.0 all-gather.7.cloned.1.call-start
  9.9 0.7 all-gather.7.cloned.1.call-update
  10.6 78.2 %all-gather.9.cloned.1.call-done = bf16[16,12,7168]{2,1,0:T(8,128)(2,1)} async-done(((bf16[1,12,7168]{2,1,0:T(8,128)(2,1)}), bf16[16,12,7168]{2,1,0:T(8,128)(2,1)}) %all-gather.9.cloned.1.call-update) | async-done | bytes 2752528 | tf_op jit(solution)/shard_map/all_gather | solution.py:19
  88.8 4.5 %reshape.35 = bf16[192,7168,1]{1,0,2:T(8,128)(2,1)} reshape(bf16[16,12,7168]{2,1,0:T(8,128)(2,1)} %all-gather.9.cloned.1.call-done) | data formatting | bytes 5505024
  93.3 57.5 %all-gather.5.cloned.1.call-done = bf16[2,7168,128]{2,1,0:T(8,128)(2,1)} async-done(((bf16[2,224,128]{2,1,0:T(8,128)(2,1)}), bf16[2,7168,128]{2,1,0:T(8,128)(2,1)}) %all-gather.5.cloned.1.call-update) | async-done | bytes 3670032 | tf_op jit(solution)/shard_map/all_gather | solution.py:20
  150.7 3.8 %convolution_bitcast_fusion = f32[2,192,128]{2,1,0:T(8,128)S(1)} fusion(bf16[192,7168,1]{1,0,2:T(8,128)(2,1)} %reshape.35, bf16[2,7168,128]{2,1,0:T(8,128)(2,1)} %all-gather.5.cloned.1.call-done), kind=kOutput, calls=%fused_computation.4 | convolution fusion | flops 704643072 | bytes 6619136 | tf_op jit(solution)/shard_map/rd,gdf->grf/dot_general | solution.py:22
  154.5 57.5 %all-gather.7.cloned.1.call-done = bf16[128,7168]{0,1:T(8,128)(2,1)} async-done(((bf16[128,224]{0,1:T(8,128)(2,1)}), bf16[128,7168]{0,1:T(8,128)(2,1)}) %all-gather.7.cloned.1.call-update) | async-done | bytes 1835024 | tf_op jit(solution)/shard_map/all_gather | solution.py:21
  212.0 3.9 %convolution_convert_fusion = bf16[192,7168]{1,0:T(8,128)(2,1)} fusion(bf16[128,7168]{0,1:T(8,128)(2,1)} %all-gather.7.cloned.1.call-done, f32[2,192,128]{2,1,0:T(8,128)S(1)} %convolution_bitcast_fusion), kind=kOutput, calls=%fused_computation | convolution fusion | flops 353845248 | bytes 4784128 | tf_op jit(solution)/shard_map/dot_general | solution.py:24
  215.9 46.2 %fusion = bf16[16,7168]{1,0:T(8,128)(2,1)S(1)} fusion(bf16[192,7168]{1,0:T(8,128)(2,1)} %convolution_convert_fusion), kind=kCustom, calls=%all-reduce-scatter | all-reduce-scatter fusion | flops 1835009 | bytes 2983936
  262.1 5.4 %collective-permute-start = (bf16[16,7168]{1,0:T(8,128)(2,1)S(1)}, bf16[16,7168]{1,0:T(8,128)(2,1)S(1)}, u32[]{:S(2)}, u32[]{:S(2)}) collective-permute-start(bf16[16,7168]{1,0:T(8,128)(2,1)S(1)} %fusion), channel_id=1, source_target_pairs={{0,1},{1,2},{2,3},{3,4},{4,5},{5,6},{6,7},{7,8},{8,9},{9,10},{10,1... | collective-permute-start | bytes 688136
  267.6 2.4 collective-permute-start.1
  270.0 6.7 %collective-permute-start.2 = (bf16[16,7168]{1,0:T(8,128)(2,1)S(1)}, bf16[16,7168]{1,0:T(8,128)(2,1)}, u32[]{:S(2)}, u32[]{:S(2)}) collective-permute-start(bf16[16,7168]{1,0:T(8,128)(2,1)S(1)} %fusion), channel_id=1, source_target_pairs={{0,3},{1,4},{2,5},{3,6},{4,7},{5,8},{6,9},{7,10},{8,11},{9,12},{10... | collective-permute-start | bytes 688136
  276.7 0.1 slice.10
  276.7 4.6 %collective-permute-start.3 = (bf16[12,7168]{1,0:T(8,128)(2,1)S(1)}, bf16[12,7168]{1,0:T(8,128)(2,1)S(1)}, u32[]{:S(2)}, u32[]{:S(2)}) collective-permute-start(bf16[12,7168]{1,0:T(8,128)(2,1)S(1)} %slice.10), channel_id=1, source_target_pairs={{0,4},{1,5},{2,6},{3,7},{4,8},{5,9},{6,10},{7,11},{8,12},{9,13},{1... | collective-permute-start | bytes 516104
  281.3 1.3 dynamic-slice.4
  283.2 32.7 %collective-permute-done.3 = bf16[12,7168]{1,0:T(8,128)(2,1)S(1)} collective-permute-done((bf16[12,7168]{1,0:T(8,128)(2,1)S(1)}, bf16[12,7168]{1,0:T(8,128)(2,1)S(1)}, u32[]{:S(2)}, u32[]{:S(2)}) %collective-permute-start.3) | collective-permute-done | bytes 172064
  315.9 0.0 copy-start.2
  315.9 0.0 collective-permute-done
  315.9 0.0 collective-permute-done.1
  315.9 0.7 copy-done.2
  316.6 0.0 copy-start.1
  316.6 0.7 copy-done.1
  317.3 0.0 collective-permute-done.2
  317.3 7.8 %concatenate = bf16[76,7168]{1,0:T(8,128)(2,1)S(1)} concatenate(bf16[12,7168]{1,0:T(8,128)(2,1)} %copy-done.2, bf16[16,7168]{1,0:T(8,128)(2,1)} %collective-permute-done.2, bf16[16,7168]{1,0:T(8,128)(2,1)} %copy-done.1, bf16[16,7168]{1,0:T(8,128)(2,1)S(1)} %collective-permute-done, bf16[16,7168]{1,0:T(8,128)(2,1)S(1)} %fusion), dimensions={0} | concatenate | bytes 2179072
  325.1 2.9 convolution_convert_fusion.1
  (2 shorter events, 0.0 us)
Async XLA Ops:
  6.5 1.5 copy-start
  6.5 82.2 %all-gather.9.cloned.1.call-start = ((), (), s32[]{:S(2)}) async-start(), calls=%async_computation.2 | async-start | bytes 3899392 | tf_op jit(solution)/shard_map/all_gather | solution.py:19
  9.1 141.6 %all-gather.5.cloned.1.call-start = ((), (), s32[]{:S(2)}) async-start(), calls=%async_computation | async-start | bytes 3784704 | tf_op jit(solution)/shard_map/all_gather | solution.py:20
  9.9 202.1 %all-gather.7.cloned.1.call-start = ((), (), s32[]{:S(2)}) async-start(), calls=%async_computation.1 | async-start | bytes 1892352 | tf_op jit(solution)/shard_map/all_gather | solution.py:21
  262.1 53.8 %collective-permute-start = (bf16[16,7168]{1,0:T(8,128)(2,1)S(1)}, bf16[16,7168]{1,0:T(8,128)(2,1)S(1)}, u32[]{:S(2)}, u32[]{:S(2)}) collective-permute-start(bf16[16,7168]{1,0:T(8,128)(2,1)S(1)} %fusion), channel_id=1, source_target_pairs={{0,1},{1,2},{2,3},{3,4},{4,5},{5,6},{6,7},{7,8},{8,9},{9,10},{10,1... | collective-permute-start | bytes 688136
  267.6 48.4 %collective-permute-start.1 = (bf16[16,7168]{1,0:T(8,128)(2,1)S(1)}, bf16[16,7168]{1,0:T(8,128)(2,1)S(1)}, u32[]{:S(2)}, u32[]{:S(2)}) collective-permute-start(bf16[16,7168]{1,0:T(8,128)(2,1)S(1)} %fusion), channel_id=1, source_target_pairs={{0,2},{1,3},{2,4},{3,5},{4,6},{5,7},{6,8},{7,9},{8,10},{9,11},{10,... | collective-permute-start | bytes 688136
  270.0 47.4 %collective-permute-start.2 = (bf16[16,7168]{1,0:T(8,128)(2,1)S(1)}, bf16[16,7168]{1,0:T(8,128)(2,1)}, u32[]{:S(2)}, u32[]{:S(2)}) collective-permute-start(bf16[16,7168]{1,0:T(8,128)(2,1)S(1)} %fusion), channel_id=1, source_target_pairs={{0,3},{1,4},{2,5},{3,6},{4,7},{5,8},{6,9},{7,10},{8,11},{9,12},{10... | collective-permute-start | bytes 688136
  276.7 39.2 %collective-permute-start.3 = (bf16[12,7168]{1,0:T(8,128)(2,1)S(1)}, bf16[12,7168]{1,0:T(8,128)(2,1)S(1)}, u32[]{:S(2)}, u32[]{:S(2)}) collective-permute-start(bf16[12,7168]{1,0:T(8,128)(2,1)S(1)} %slice.10), channel_id=1, source_target_pairs={{0,4},{1,5},{2,6},{3,7},{4,8},{5,9},{6,10},{7,11},{8,12},{9,13},{1... | collective-permute-start | bytes 516104
  315.9 0.7 copy-start.2
  316.6 0.7 copy-start.1
Sparse Core Ops, SparseCore 0:
  9.4 79.3 all-gather.8
  92.0 58.7 all-gather.4
  153.9 58.0 all-gather.6
where the time goes:
time: 335 us
  waiting for transfers between devices  227 us (68%)
  blocking collectives  46.2 us (14%)
  starting transfers between devices  19.2 us (6%)
  local copies, waits for them, and re-layouts  15.3 us (5%)
  between operations  13.8 us (4%)
  matrix products  11.6 us (3%)
    all_gather x1, waiting for transfers between devices, body(): dispatched = lax.all_gather(packed, 'expert', axis=0, tiled=True)  78.2 us
    all_gather x1, waiting for transfers between devices, body(): dn = lax.all_gather(down_weight, 'dp', axis=1, tiled=True)  57.5 us
    all_gather x1, waiting for transfers between devices, body(): gu = lax.all_gather(gate_up, 'dp', axis=1, tiled=True)  57.5 us
    unnamed x1, blocking collectives  46.2 us
    unnamed x7, waiting for transfers between devices  34.1 us
    unnamed x4, starting transfers between devices  19.1 us
    unnamed x10, local copies, waits for them, and re-layouts  15.2 us
  transfers between devices with their start and end apart: 7, of which 4 were waited for; matrix products, arithmetic and copies ran while one was open for 3% of the time, Pallas kernels for 0%

commit v1 on v0

--- a/solution.py
+++ b/solution.py
@@ -1,3 +1,4 @@
+import functools
 import jax
 import jax.numpy as jnp
 from jax import lax
@@ -5,6 +6,21 @@
 
 EXPERTS = 1
 CAP = 12
+
+
+def prepare_cells(values, axis_id):
+    return jnp.concatenate(
+        jax.lax.all_to_all(
+            jnp.stack([values for _ in range(jax.lax.axis_size(axis_id))]),
+            concat_axis=0,
+            split_axis=0,
+            axis_name=axis_id,
+        ),
+        axis=0,
+    )
+
+
+ranges_wait = functools.partial(prepare_cells, axis_id="expert")
 
 
 def body(tokens, route_ids, route_gates, gate_up, down_weight):
@@ -16,7 +32,7 @@
     capacity_ids = jnp.arange(CAP, dtype=jnp.int32)
     packing = (routed[None, :] & (places[None, :] == capacity_ids[:, None])).astype(jnp.bfloat16)
     packed = jnp.dot(packing, tokens, preferred_element_type=jnp.float32).astype(jnp.bfloat16)
-    dispatched = lax.all_gather(packed, "expert", axis=0, tiled=True)
+    dispatched = ranges_wait(packed)
     gu = lax.all_gather(gate_up, "dp", axis=1, tiled=True)
     dn = lax.all_gather(down_weight, "dp", axis=1, tiled=True)
     projected = jnp.einsum("rd,gdf->grf", dispatched, gu, preferred_element_type=jnp.float32)

time: 335 us -> 314 us (0.937)
  the two profiles are of different devices: /device:TPU:96 before, /device:TPU:120 now
where the time goes in v1:
time: 314 us; the launch traced here: 313 us
  waiting for transfers between devices  192 us (61%)
  blocking collectives  44.2 us (14%)
  starting transfers between devices  33.3 us (11%)
  local copies, waits for them, and re-layouts  17.6 us (6%)
  between operations  14.2 us (5%)
  matrix products  10.9 us (3%)
    all_to_all x1, waiting for transfers between devices, prepare_cells(): jax.lax.all_to_all(jnp.stack([values for _ in range(jax.lax.axis_size(axi...  159 us
    unnamed x1, blocking collectives  44.2 us
    unnamed x6, waiting for transfers between devices  32.9 us
    unnamed x4, starting transfers between devices  18.9 us
    all_to_all x1, starting transfers between devices, prepare_cells(): jax.lax.all_to_all(jnp.stack([values for _ in range(jax.lax.axis_size(axi...  14.3 us
    unnamed x9, local copies, waits for them, and re-layouts  10.7 us
  transfers between devices with their start and end apart: 7, of which 2 were waited for; matrix products, arithmetic and copies ran while one was open for 3% of the time, Pallas kernels for 0%

profile of v1, /device:TPU:120, one launch (start us, length us, event | category | flops | bytes accessed | tf_op | source)
XLA Modules:
  0.0 313.4 jit_solution(3588339475697003379)
XLA Ops:
  6.5 0.0 copy-start
  6.5 0.9 select_reduce_fusion
  7.4 0.1 copy.8
  7.5 0.2 reduce-window.7
  7.7 0.1 add_reduce_fusion
  7.8 0.3 copy-done
  8.1 0.3 convolution_convert_fusion.2
  8.4 2.3 stack.2
  10.7 14.3 %all-to-all-start = ((bf16[16,12,7168]{2,1,0:T(8,128)(2,1)}), bf16[16,12,7168]{2,1,0:T(8,128)(2,1)}, u32[]{:S(2)}, u32[]{:S(2)}) async-start(bf16[16,12,7168]{2,1,0:T(8,128)(2,1)} %stack.2), calls=%async_computation | async-start | bytes 7340032 | tf_op jit(solution)/shard_map/all_to_all | solution.py:13
  25.0 0.0 all-gather.3.cloned.1.call-start
  25.1 0.7 all-gather.3.cloned.1.call-update
  25.8 0.0 all-gather.5.cloned.1.call-start
  25.8 0.7 all-gather.5.cloned.1.call-update
  26.5 159.2 %all-to-all-done = bf16[16,12,7168]{2,1,0:T(8,128)(2,1)} async-done(((bf16[16,12,7168]{2,1,0:T(8,128)(2,1)}), bf16[16,12,7168]{2,1,0:T(8,128)(2,1)}, u32[]{:S(2)}, u32[]{:S(2)}) %all-to-all-start) | async-done | bytes 2752544 | tf_op jit(solution)/shard_map/all_to_all | solution.py:13
  185.7 4.5 %reshape.39 = bf16[192,7168,1]{1,0,2:T(8,128)(2,1)} reshape(bf16[16,12,7168]{2,1,0:T(8,128)(2,1)} %all-to-all-done) | data formatting | bytes 5505024 | tf_op jit(solution)/shard_map/reshape | solution.py:12
  190.2 0.0 all-gather.3.cloned.1.call-done
  190.2 3.8 %convolution_bitcast_fusion = f32[2,192,128]{2,1,0:T(8,128)S(1)} fusion(bf16[192,7168,1]{1,0,2:T(8,128)(2,1)} %reshape.39, bf16[2,7168,128]{2,1,0:T(8,128)(2,1)} %all-gather.3.cloned.1.call-done), kind=kOutput, calls=%fused_computation.3 | convolution fusion | flops 704643072 | bytes 6619136 | tf_op jit(solution)/shard_map/rd,gdf->grf/dot_general | solution.py:38
  193.9 0.0 all-gather.5.cloned.1.call-done
  193.9 3.9 %convolution_convert_fusion = bf16[192,7168]{1,0:T(8,128)(2,1)} fusion(bf16[128,7168]{0,1:T(8,128)(2,1)} %all-gather.5.cloned.1.call-done, f32[2,192,128]{2,1,0:T(8,128)S(1)} %convolution_bitcast_fusion), kind=kOutput, calls=%fused_computation | convolution fusion | flops 353845248 | bytes 4784128 | tf_op jit(solution)/shard_map/dot_general | solution.py:40
  197.9 44.2 %fusion = bf16[16,7168]{1,0:T(8,128)(2,1)S(1)} fusion(bf16[192,7168]{1,0:T(8,128)(2,1)} %convolution_convert_fusion), kind=kCustom, calls=%all-reduce-scatter | all-reduce-scatter fusion | flops 1835009 | bytes 2983936
  242.1 5.3 %collective-permute-start = (bf16[16,7168]{1,0:T(8,128)(2,1)S(1)}, bf16[16,7168]{1,0:T(8,128)(2,1)S(1)}, u32[]{:S(2)}, u32[]{:S(2)}) collective-permute-start(bf16[16,7168]{1,0:T(8,128)(2,1)S(1)} %fusion), channel_id=1, source_target_pairs={{0,1},{1,2},{2,3},{3,4},{4,5},{5,6},{6,7},{7,8},{8,9},{9,10},{10,1... | collective-permute-start | bytes 688136
  247.3 3.4 %collective-permute-start.1 = (bf16[16,7168]{1,0:T(8,128)(2,1)S(1)}, bf16[16,7168]{1,0:T(8,128)(2,1)S(1)}, u32[]{:S(2)}, u32[]{:S(2)}) collective-permute-start(bf16[16,7168]{1,0:T(8,128)(2,1)S(1)} %fusion), channel_id=1, source_target_pairs={{0,2},{1,3},{2,4},{3,5},{4,6},{5,7},{6,8},{7,9},{8,10},{9,11},{10,... | collective-permute-start | bytes 688136
  250.7 6.7 %collective-permute-start.2 = (bf16[16,7168]{1,0:T(8,128)(2,1)S(1)}, bf16[16,7168]{1,0:T(8,128)(2,1)}, u32[]{:S(2)}, u32[]{:S(2)}) collective-permute-start(bf16[16,7168]{1,0:T(8,128)(2,1)S(1)} %fusion), channel_id=1, source_target_pairs={{0,3},{1,4},{2,5},{3,6},{4,7},{5,8},{6,9},{7,10},{8,11},{9,12},{10... | collective-permute-start | bytes 688136
  257.4 0.1 slice.10
  257.5 3.6 %collective-permute-start.3 = (bf16[12,7168]{1,0:T(8,128)(2,1)S(1)}, bf16[12,7168]{1,0:T(8,128)(2,1)S(1)}, u32[]{:S(2)}, u32[]{:S(2)}) collective-permute-start(bf16[12,7168]{1,0:T(8,128)(2,1)S(1)} %slice.10), channel_id=1, source_target_pairs={{0,4},{1,5},{2,6},{3,7},{4,8},{5,9},{6,10},{7,11},{8,12},{9,13},{1... | collective-permute-start | bytes 516104
  261.1 1.3 dynamic-slice.4
  263.0 31.6 %collective-permute-done.3 = bf16[12,7168]{1,0:T(8,128)(2,1)S(1)} collective-permute-done((bf16[12,7168]{1,0:T(8,128)(2,1)S(1)}, bf16[12,7168]{1,0:T(8,128)(2,1)S(1)}, u32[]{:S(2)}, u32[]{:S(2)}) %collective-permute-start.3) | collective-permute-done | bytes 172064
  294.6 0.0 copy-start.2
  294.6 0.0 collective-permute-done
  294.6 0.0 collective-permute-done.1
  294.6 0.7 copy-done.2
  295.3 0.0 copy-start.1
  295.3 0.7 copy-done.1
  295.9 0.0 collective-permute-done.2
  295.9 7.8 %concatenate = bf16[76,7168]{1,0:T(8,128)(2,1)S(1)} concatenate(bf16[12,7168]{1,0:T(8,128)(2,1)} %copy-done.2, bf16[16,7168]{1,0:T(8,128)(2,1)} %collective-permute-done.2, bf16[16,7168]{1,0:T(8,128)(2,1)} %copy-done.1, bf16[16,7168]{1,0:T(8,128)(2,1)S(1)} %collective-permute-done, bf16[16,7168]{1,0:T(8,128)(2,1)S(1)} %fusion), dimensions={0} | concatenate | bytes 2179072
  303.7 2.9 convolution_convert_fusion.1
  (2 shorter events, 0.0 us)
Async XLA Ops:
  6.5 1.5 copy-start
  10.7 175.0 %all-to-all-start = ((bf16[16,12,7168]{2,1,0:T(8,128)(2,1)}), bf16[16,12,7168]{2,1,0:T(8,128)(2,1)}, u32[]{:S(2)}, u32[]{:S(2)}) async-start(bf16[16,12,7168]{2,1,0:T(8,128)(2,1)} %stack.2), calls=%async_computation | async-start | bytes 7340032 | tf_op jit(solution)/shard_map/all_to_all | solution.py:13
  25.0 165.1 %all-gather.3.cloned.1.call-start = ((), (), s32[]{:S(2)}) async-start(), calls=%async_computation.1 | async-start | bytes 3784704 | tf_op jit(solution)/shard_map/all_gather | solution.py:36
  25.8 168.2 %all-gather.5.cloned.1.call-start = ((), (), s32[]{:S(2)}) async-start(), calls=%async_computation.2 | async-start | bytes 1892352 | tf_op jit(solution)/shard_map/all_gather | solution.py:37
  242.1 52.5 %collective-permute-start = (bf16[16,7168]{1,0:T(8,128)(2,1)S(1)}, bf16[16,7168]{1,0:T(8,128)(2,1)S(1)}, u32[]{:S(2)}, u32[]{:S(2)}) collective-permute-start(bf16[16,7168]{1,0:T(8,128)(2,1)S(1)} %fusion), channel_id=1, source_target_pairs={{0,1},{1,2},{2,3},{3,4},{4,5},{5,6},{6,7},{7,8},{8,9},{9,10},{10,1... | collective-permute-start | bytes 688136
  247.3 47.2 %collective-permute-start.1 = (bf16[16,7168]{1,0:T(8,128)(2,1)S(1)}, bf16[16,7168]{1,0:T(8,128)(2,1)S(1)}, u32[]{:S(2)}, u32[]{:S(2)}) collective-permute-start(bf16[16,7168]{1,0:T(8,128)(2,1)S(1)} %fusion), channel_id=1, source_target_pairs={{0,2},{1,3},{2,4},{3,5},{4,6},{5,7},{6,8},{7,9},{8,10},{9,11},{10,... | collective-permute-start | bytes 688136
  250.7 45.2 %collective-permute-start.2 = (bf16[16,7168]{1,0:T(8,128)(2,1)S(1)}, bf16[16,7168]{1,0:T(8,128)(2,1)}, u32[]{:S(2)}, u32[]{:S(2)}) collective-permute-start(bf16[16,7168]{1,0:T(8,128)(2,1)S(1)} %fusion), channel_id=1, source_target_pairs={{0,3},{1,4},{2,5},{3,6},{4,7},{5,8},{6,9},{7,10},{8,11},{9,12},{10... | collective-permute-start | bytes 688136
  257.5 37.1 %collective-permute-start.3 = (bf16[12,7168]{1,0:T(8,128)(2,1)S(1)}, bf16[12,7168]{1,0:T(8,128)(2,1)S(1)}, u32[]{:S(2)}, u32[]{:S(2)}) collective-permute-start(bf16[12,7168]{1,0:T(8,128)(2,1)S(1)} %slice.10), channel_id=1, source_target_pairs={{0,4},{1,5},{2,6},{3,7},{4,8},{5,9},{6,10},{7,11},{8,12},{9,13},{1... | collective-permute-start | bytes 516104
  294.6 0.7 copy-start.2
  295.3 0.7 copy-start.1
Sparse Core Ops, SparseCore 0:
  29.0 61.3 all-gather.2
  93.5 57.9 all-gather.4
